TPU v7x, 32 devices: a whole 2x2x4 slice. The times are simulated.
32 devices in a mesh: dp: 8 (over z, x), expert: 4 (over y, core).
Axes of the slice: x: 2, y: 2, z: 4, core: 2. Of those that a mesh axis runs over, the one named last changes fastest.
Arguments:
- tokens: bfloat16 [8192, 768], P(('dp', 'expert')), may hold values from -6 to 6
- expert_ids: int32 [8192, 2], P(('dp', 'expert')), may hold values from 0 to 15, all different within a row; in each aligned block of 256 rows (0 to 255, 256 to 511, ...) at most 64 rows name the same one
- gate_fixed: int32 [8192, 2], P(('dp', 'expert')), may hold values from 8192 to 65535
- cotangent: bfloat16 [8192, 768], P(('dp', 'expert')), may hold values from -6 to 6
- w_gate: bfloat16 [16, 768, 384], P('expert'), may hold values from -0.21875 to 0.21875
- w_up: bfloat16 [16, 768, 384], P('expert'), may hold values from -0.21875 to 0.21875
- w_down: bfloat16 [16, 768, 384], P('expert'), may hold values from -0.3125 to 0.3125
Outputs:
- layer_out: bfloat16 [8192, 768], P(('dp', 'expert'))
- input_grad: bfloat16 [8192, 768], P(('dp', 'expert'))
- grad_gate: float32 [16, 768, 384], P('expert', 'dp')
- grad_up: float32 [16, 768, 384], P('expert', 'dp')
- grad_down: float32 [16, 768, 384], P('expert', 'dp')
Inputs may be any that keep to these rules, and one draw needn't show every extreme that they name: `expert_ids`: A row names 2 different experts. In each aligned block of 256 rows (the rows of one device) no expert is named by more than 64 rows, and in some block one expert is named by exactly 64 rows.
All inputs are finite; a program needn't handle non-finite values.
Results may differ from a plain program's by a relative error of at most 0.015.
Values may be sent and summed in bfloat16 or wider, within the bound.
A program may use at most 64 MiB of HBM per device.

v0:
```python
import jax
import jax.numpy as jnp
from jax import lax
from jax.sharding import PartitionSpec as P


def expert_forward(rows_in, w_gate, w_up, w_down):
    pre_gate = jnp.einsum("erd,edf->erf", rows_in, w_gate, preferred_element_type=jnp.float32)
    pre_up = jnp.einsum("erd,edf->erf", rows_in, w_up, preferred_element_type=jnp.float32)
    sigmoid_gate = jax.nn.sigmoid(pre_gate)
    activated = pre_gate * sigmoid_gate
    hidden = (activated * pre_up).astype(jnp.bfloat16)
    outputs = jnp.einsum("erf,edf->erd", hidden, w_down, preferred_element_type=jnp.float32).astype(
        jnp.bfloat16
    )
    return (outputs, (pre_gate, pre_up, sigmoid_gate, activated, hidden))


def expert_backward(rows_in, grads_in, saved_state, w_gate, w_up, w_down, grad_scale):
    pre_gate, pre_up, sigmoid_gate, activated, hidden = saved_state
    hidden_grad = jnp.einsum("erd,edf->erf", grads_in, w_down, preferred_element_type=jnp.float32)
    gate_grad = (
        hidden_grad * pre_up * sigmoid_gate * (1.0 + pre_gate * (1.0 - sigmoid_gate))
    ).astype(jnp.bfloat16)
    up_grad = (hidden_grad * activated).astype(jnp.bfloat16)
    entry_grad = (
        jnp.einsum("erf,edf->erd", gate_grad, w_gate, preferred_element_type=jnp.float32)
        + jnp.einsum("erf,edf->erd", up_grad, w_up, preferred_element_type=jnp.float32)
    ).astype(jnp.bfloat16)
    weight_gate = (
        jnp.einsum("erd,erf->edf", rows_in, gate_grad, preferred_element_type=jnp.float32)
        * grad_scale
    )
    weight_up = (
        jnp.einsum("erd,erf->edf", rows_in, up_grad, preferred_element_type=jnp.float32)
        * grad_scale
    )
    weight_down = (
        jnp.einsum("erd,erf->edf", grads_in, hidden, preferred_element_type=jnp.float32)
        * grad_scale
    )
    return (entry_grad, weight_gate, weight_up, weight_down)


def shards(tokens, expert_ids, gate_fixed, cotangent, w_gate, w_up, w_down):
    peer_count = lax.axis_size("expert")
    replicas = lax.axis_size("dp")
    local_experts = w_gate.shape[0]
    tok_rows = expert_ids.shape[0]
    top_count = expert_ids.shape[1]
    d_model = tokens.shape[1]
    experts_all = local_experts * peer_count
    entries = tok_rows * top_count
    capacity = entries * 2 // experts_all
    slots_all = experts_all * capacity
    grad_scale = float(tok_rows * replicas * top_count // local_experts) ** (-0.5)
    flat_ids = expert_ids.reshape(entries)
    onehot = (flat_ids[:, None] == jnp.arange(experts_all, dtype=jnp.int32)[None, :]).astype(
        jnp.int32
    )
    slot_rank = jnp.sum((jnp.cumsum(onehot, axis=0) - 1) * onehot, axis=1)
    owner_dev = flat_ids // local_experts
    within = flat_ids % local_experts
    slot_index = (within * peer_count + owner_dev) * capacity + slot_rank
    source = (
        jnp.full((slots_all,), entries, jnp.int32)
        .at[slot_index]
        .set(jnp.arange(entries, dtype=jnp.int32))
    )
    is_valid = source < entries
    token_of = jnp.where(is_valid, source // top_count, 0)
    gate_values = gate_fixed.reshape(entries).astype(jnp.float32) / 65536.0
    slot_gate = jnp.where(is_valid, gate_values[jnp.minimum(source, entries - 1)], 0.0)
    send_rows = jnp.where(is_valid[:, None], tokens[token_of], jnp.zeros((), jnp.bfloat16))
    send_rows = send_rows.reshape(local_experts, peer_count * capacity, d_model)
    send_grads = (slot_gate[:, None] * cotangent[token_of].astype(jnp.float32)).astype(jnp.bfloat16)
    send_grads = send_grads.reshape(local_experts, peer_count * capacity, d_model)
    rows_in = lax.all_to_all(send_rows, "expert", split_axis=1, concat_axis=1, tiled=True)
    outputs, saved_state = expert_forward(rows_in, w_gate, w_up, w_down)
    back_out = lax.all_to_all(outputs, "expert", split_axis=1, concat_axis=1, tiled=True)
    grads_in = lax.all_to_all(send_grads, "expert", split_axis=1, concat_axis=1, tiled=True)
    entry_grad, weight_gate, weight_up, weight_down = expert_backward(
        rows_in, grads_in, saved_state, w_gate, w_up, w_down, grad_scale
    )
    back_in = lax.all_to_all(entry_grad, "expert", split_axis=1, concat_axis=1, tiled=True)

    def combine(returned, weights):
        picked = returned.reshape(slots_all, d_model)[slot_index].astype(jnp.float32)
        summed = jnp.sum((weights[:, None] * picked).reshape(tok_rows, top_count, d_model), axis=1)
        return summed.astype(jnp.bfloat16)

    layer_out = combine(back_out, gate_values)
    input_grad = combine(back_in, jnp.ones_like(gate_values))
    grad_gate, grad_up, grad_down = (
        lax.psum_scatter(
            weight_gate.astype(jnp.bfloat16), "dp", scatter_dimension=1, tiled=True
        ).astype(jnp.float32),
        lax.psum_scatter(
            weight_up.astype(jnp.bfloat16), "dp", scatter_dimension=1, tiled=True
        ).astype(jnp.float32),
        lax.psum_scatter(
            weight_down.astype(jnp.bfloat16), "dp", scatter_dimension=1, tiled=True
        ).astype(jnp.float32),
    )
    return (layer_out, input_grad, grad_gate, grad_up, grad_down)


def solution(mesh):
    return jax.shard_map(
        shards,
        mesh=mesh,
        in_specs=(
            P(("dp", "expert"), None),
            P(("dp", "expert"), None),
            P(("dp", "expert"), None),
            P(("dp", "expert"), None),
            P("expert", None, None),
            P("expert", None, None),
            P("expert", None, None),
        ),
        out_specs=(
            P(("dp", "expert"), None),
            P(("dp", "expert"), None),
            P("expert", "dp", None),
            P("expert", "dp", None),
            P("expert", "dp", None),
        ),
        check_vma=False,
    )
```

profile of v0, /device:TPU:0, one launch (start us, length us, event | category | flops | bytes accessed | tf_op | source)
XLA Modules:
  0.0 315.9 jit_solution(13793462235881466038)
XLA Ops:
  7.2 0.0 copy-start
  7.2 1.0 copy.44
  8.1 0.1 eq.31
  8.3 0.1 eq.27
  8.4 0.1 reshape.196
  8.6 0.7 convert_multiply_fusion
  9.3 0.1 copy.43
  9.4 0.1 div.43
  9.6 1.2 reduce-window.6
  10.7 0.2 slice_reduce_fusion
  11.0 0.1 fusion.3
  11.1 2.4 scatter_custom_fusion
  13.6 0.0 copy-start.1
  13.6 6.9 %gather_fusion.2 = f32[1024]{0:T(1024)S(1)} fusion(f32[512]{0:T(512)S(1)} %div.43, s32[1024]{0:T(1024)S(1)} %fusion.8), kind=kCustom, calls=%fused_computation.2 | custom fusion | bytes 12288 | tf_op jit(solution)/shard_map/gather | solution.py:73
  20.5 0.2 copy.48
  20.7 5.2 %gather_fusion = bf16[1024,768]{1,0:T(8,128)(2,1)} fusion(bf16[256,768]{1,0:T(8,128)(2,1)S(1)} %copy-done.1, s32[1024]{0:T(1024)S(1)} %fusion.7), kind=kCustom, calls=%fused_computation | custom fusion | bytes 3149824 | tf_op jit(solution)/shard_map/gather | solution.py:74
  25.9 3.8 %copy_select_fusion = bf16[4,256,768]{2,0,1:T(4,128)(2,1)} fusion(bf16[4,256,768]{2,1,0:T(8,128)(2,1)} %bitcast.43, pred[4,256]{0,1:T(8,128)(4,1)S(1)} %copy.48), kind=kLoop, calls=%fused_computation.13 | loop fusion | flops 786432 | bytes 3146752 | tf_op jit(solution)/shard_map/jit(_where)/select_n | solution.py:74
  29.8 4.5 %all-to-all-start = ((bf16[4,256,768]{2,0,1:T(4,128)(2,1)}), bf16[4,256,768]{2,0,1:T(4,128)(2,1)}, u32[]{:S(2)}, u32[]{:S(2)}) async-start(bf16[4,256,768]{2,0,1:T(4,128)(2,1)} %copy_select_fusion), calls=%async_computation | async-start | bytes 3145728 | tf_op jit(solution)/shard_map/all_to_all | solution.py:78
  34.3 0.1 copy.55
  34.4 0.0 copy-done.2
  34.4 5.2 %gather_fusion.3 = bf16[1024,768]{1,0:T(8,128)(2,1)} fusion(bf16[256,768]{1,0:T(8,128)(2,1)S(1)} %copy-done.2, s32[1024]{0:T(1024)S(1)} %fusion.7), kind=kCustom, calls=%fused_computation.3 | custom fusion | bytes 3149824 | tf_op jit(solution)/shard_map/gather | solution.py:76
  39.6 1.7 convert.3
  41.3 3.2 %fusion = bf16[4,256,768]{2,0,1:T(4,128)(2,1)} fusion(f32[4,256,768]{2,1,0:T(8,128)S(1)} %convert.3, f32[4,256]{0,1:T(8,128)S(1)} %copy.55), kind=kLoop, calls=%fused_computation.10 | loop fusion | flops 1572864 | bytes 4722688 | tf_op jit(solution)/shard_map/convert_element_type | solution.py:76
  44.6 10.6 %all-to-all-done = bf16[4,256,768]{2,0,1:T(4,128)(2,1)} async-done(((bf16[4,256,768]{2,0,1:T(4,128)(2,1)}), bf16[4,256,768]{2,0,1:T(4,128)(2,1)}, u32[]{:S(2)}, u32[]{:S(2)}) %all-to-all-start) | async-done | bytes 1572896 | tf_op jit(solution)/shard_map/all_to_all | solution.py:78
  55.1 4.3 %all-to-all-start.2 = ((bf16[4,256,768]{2,0,1:T(4,128)(2,1)}), bf16[4,256,768]{2,0,1:T(4,128)(2,1)}, u32[]{:S(2)}, u32[]{:S(2)}) async-start(bf16[4,256,768]{2,0,1:T(4,128)(2,1)} %fusion), calls=%async_computation.2 | async-start | bytes 3145728 | tf_op jit(solution)/shard_map/all_to_all | solution.py:81
  59.4 0.2 reduce-scatter.8.cloned.1.call-start
  59.7 3.8 %copy.60 = bf16[4,256,768]{1,2,0:T(8,128)(2,1)} copy(bf16[4,256,768]{2,0,1:T(4,128)(2,1)} %all-to-all-done) | data formatting | bytes 3145728 | tf_op jit(solution)/shard_map/all_to_all | solution.py:78
  63.4 4.5 %fusion.15 = f32[4,256,384]{2,1,0:T(8,128)} fusion(bf16[4,256,768]{1,2,0:T(8,128)(2,1)} %copy.60, bf16[4,768,384]{2,1,0:T(8,128)(2,1)} %param.12), kind=kOutput, calls=%fused_computation.55 | convolution fusion | flops 603979776 | bytes 5505024 | tf_op jit(solution)/shard_map/erd,edf->erf/dot_general | solution.py:9
  67.9 2.2 fusion.14
  70.1 9.4 %all-to-all-done.2 = bf16[4,256,768]{2,0,1:T(4,128)(2,1)} async-done(((bf16[4,256,768]{2,0,1:T(4,128)(2,1)}), bf16[4,256,768]{2,0,1:T(4,128)(2,1)}, u32[]{:S(2)}, u32[]{:S(2)}) %all-to-all-start.2) | async-done | bytes 1572896 | tf_op jit(solution)/shard_map/all_to_all | solution.py:81
  79.6 3.8 %copy.62 = bf16[4,256,768]{1,2,0:T(8,128)(2,1)} copy(bf16[4,256,768]{2,0,1:T(4,128)(2,1)} %all-to-all-done.2) | data formatting | bytes 3145728 | tf_op jit(solution)/shard_map/all_to_all | solution.py:81
  83.3 4.8 %multiply_convert_fusion.3 = (bf16[4,256,384]{2,1,0:T(8,128)(2,1)}, bf16[4,256,384]{2,1,0:T(8,128)(2,1)S(1)}, bf16[4,256,384]{2,1,0:T(8,128)(2,1)S(1)}) fusion(f32[4,256,384]{2,1,0:T(8,128)} %fusion.14, f32[4,256,384]{2,1,0:T(8,128)} %fusion.15, bf16[4,256,768]{1,2,0:T(8,128)(2,1)} %copy.62, bf16[4,768,384]{2,1,0:T(8,128)(2,1)S(1)} %copy-done), kind=kOutput, calls=%fused_computation.14 | convolution fusion | flops 609878016 | bytes 9437184 | tf_op jit(solution)/shard_map/erd,edf->erf/dot_general | solution.py:21
  88.2 1.0 copy-done.7
  89.2 2.4 multiply_convert_fusion
  91.6 0.0 reduce-scatter.8.cloned.1.call-update
  91.6 0.0 reduce-scatter.6.cloned.1.call-start
  91.7 4.0 %multiply_convert_fusion.1 = bf16[4,768,384]{2,1,0:T(8,128)(2,1)} fusion(bf16[4,256,768]{1,2,0:T(8,128)(2,1)} %copy.60, bf16[4,256,384]{2,1,0:T(8,128)(2,1)} %get-tuple-element.7), kind=kOutput, calls=%fused_computation.7 | convolution fusion | flops 606339072 | bytes 4718592 | tf_op jit(solution)/shard_map/erd,erf->edf/dot_general | solution.py:35
  95.6 0.0 reduce-scatter.6.cloned.1.call-update
  95.7 0.0 reduce-scatter.4.cloned.1.call-start
  95.7 3.8 %multiply_convert_fusion.2 = bf16[4,768,384]{2,1,0:T(8,128)(2,1)} fusion(bf16[4,256,768]{1,2,0:T(8,128)(2,1)} %copy.60, bf16[4,256,384]{2,1,0:T(8,128)(2,1)S(1)} %get-tuple-element.8), kind=kOutput, calls=%fused_computation.8 | convolution fusion | flops 606339072 | bytes 4718592 | tf_op jit(solution)/shard_map/erd,erf->edf/dot_general | solution.py:31
  99.5 0.0 reduce-scatter.4.cloned.1.call-update
  99.6 2.2 convolution_convert_fusion
  101.7 2.4 copy.52
  104.1 4.4 %all-to-all-start.1 = ((bf16[4,256,768]{2,0,1:T(4,128)(2,1)}), bf16[4,256,768]{2,0,1:T(4,128)(2,1)}, u32[]{:S(2)}, u32[]{:S(2)}) async-start(bf16[4,256,768]{2,0,1:T(4,128)(2,1)} %copy.52), calls=%async_computation.1 | async-start | bytes 3145728 | tf_op jit(solution)/shard_map/all_to_all | solution.py:80
  108.5 0.0 copy-start.5
  108.5 2.8 fusion.16
  111.4 1.0 add_convert_fusion
  112.4 2.4 copy.58
  114.8 13.8 %all-to-all-done.1 = bf16[4,256,768]{2,0,1:T(4,128)(2,1)} async-done(((bf16[4,256,768]{2,0,1:T(4,128)(2,1)}), bf16[4,256,768]{2,0,1:T(4,128)(2,1)}, u32[]{:S(2)}, u32[]{:S(2)}) %all-to-all-start.1) | async-done | bytes 1572896 | tf_op jit(solution)/shard_map/all_to_all | solution.py:80
  128.6 4.6 %all-to-all-start.3 = ((bf16[4,256,768]{2,0,1:T(4,128)(2,1)}), bf16[4,256,768]{2,0,1:T(4,128)(2,1)}, u32[]{:S(2)}, u32[]{:S(2)}) async-start(bf16[4,256,768]{2,0,1:T(4,128)(2,1)} %copy.58), calls=%async_computation.3 | async-start | bytes 3145728 | tf_op jit(solution)/shard_map/all_to_all | solution.py:85
  133.2 2.9 copy.53
  136.1 4.0 %gather_fusion.1 = bf16[512,768]{1,0:T(8,128)(2,1)S(1)} fusion(bf16[1024,768]{1,0:T(8,128)(2,1)} %bitcast.42, s32[1024]{0:T(1024)S(1)} %pad_clamp_fusion), kind=kCustom, calls=%fused_computation.1 | custom fusion | bytes 1574912 | tf_op jit(solution)/shard_map/gather | solution.py:88
  140.1 2.0 reshape.200
  142.0 11.3 %all-to-all-done.3 = bf16[4,256,768]{2,0,1:T(4,128)(2,1)} async-done(((bf16[4,256,768]{2,0,1:T(4,128)(2,1)}), bf16[4,256,768]{2,0,1:T(4,128)(2,1)}, u32[]{:S(2)}, u32[]{:S(2)}) %all-to-all-start.3) | async-done | bytes 1572896 | tf_op jit(solution)/shard_map/all_to_all | solution.py:85
  153.3 2.8 copy.59
  156.1 4.7 %gather_fusion.4 = bf16[512,768]{1,0:T(8,128)(2,1)} fusion(bf16[1024,768]{1,0:T(8,128)(2,1)} %bitcast.41, s32[1024]{0:T(1024)S(1)} %pad_clamp_fusion), kind=kCustom, calls=%fused_computation.4 | custom fusion | bytes 1574912 | tf_op jit(solution)/shard_map/gather | solution.py:88
  160.8 2.2 gather.25
  162.9 2.8 reduce_sum.35
  165.8 4.2 %multiply_reduce_fusion = bf16[256,768]{1,0:T(8,128)(2,1)} fusion(f32[256,2,768]{2,1,0:T(2,128)} %reshape.200, f32[256,2]{1,0:T(8,128)S(1)} %copy.43), kind=kLoop, calls=%fused_computation.16 | loop fusion | flops 589824 | bytes 1968128 | tf_op jit(solution)/shard_map/reduce_sum | solution.py:89
  169.9 1.8 convert_element_type.88
  171.7 63.0 %reduce-scatter.6.cloned.1.call-done = bf16[4,96,384]{2,1,0:T(8,128)(2,1)} async-done(((bf16[4,768,384]{2,1,0:T(8,128)(2,1)}), bf16[4,96,384]{2,1,0:T(8,128)(2,1)}) %reduce-scatter.6.cloned.1.call-update) | async-done | bytes 294928 | tf_op jit(solution)/shard_map/reduce_scatter | solution.py:98
  234.8 1.8 convert_element_type.86
  236.6 70.9 %reduce-scatter.4.cloned.1.call-done = bf16[4,96,384]{2,1,0:T(8,128)(2,1)} async-done(((bf16[4,768,384]{2,1,0:T(8,128)(2,1)}), bf16[4,96,384]{2,1,0:T(8,128)(2,1)}) %reduce-scatter.4.cloned.1.call-update) | async-done | bytes 294928 | tf_op jit(solution)/shard_map/reduce_scatter | solution.py:95
  307.5 1.8 convert_element_type.84
  (25 shorter events, 0.2 us)
Async XLA Ops:
  7.2 76.2 %copy-start = (bf16[4,768,384]{2,1,0:T(8,128)(2,1)S(1)}, bf16[4,768,384]{2,1,0:T(8,128)(2,1)}, u32[]{:S(2)}) copy-start(bf16[4,768,384]{2,1,0:T(8,128)(2,1)} %param.13) | copy-start | bytes 7077892
  13.6 7.1 %copy-start.1 = (bf16[256,768]{1,0:T(8,128)(2,1)S(1)}, bf16[256,768]{1,0:T(8,128)(2,1)}, u32[]{:S(2)}) copy-start(bf16[256,768]{1,0:T(8,128)(2,1)} %param.7) | copy-start | bytes 1179652
  29.8 4.6 %copy-start.2 = (bf16[256,768]{1,0:T(8,128)(2,1)S(1)}, bf16[256,768]{1,0:T(8,128)(2,1)}, u32[]{:S(2)}) copy-start(bf16[256,768]{1,0:T(8,128)(2,1)} %param.10) | copy-start | bytes 1179652
  29.8 25.3 %all-to-all-start = ((bf16[4,256,768]{2,0,1:T(4,128)(2,1)}), bf16[4,256,768]{2,0,1:T(4,128)(2,1)}, u32[]{:S(2)}, u32[]{:S(2)}) async-start(bf16[4,256,768]{2,0,1:T(4,128)(2,1)} %copy_select_fusion), calls=%async_computation | async-start | bytes 3145728 | tf_op jit(solution)/shard_map/all_to_all | solution.py:78
  55.1 24.5 %all-to-all-start.2 = ((bf16[4,256,768]{2,0,1:T(4,128)(2,1)}), bf16[4,256,768]{2,0,1:T(4,128)(2,1)}, u32[]{:S(2)}, u32[]{:S(2)}) async-start(bf16[4,256,768]{2,0,1:T(4,128)(2,1)} %fusion), calls=%async_computation.2 | async-start | bytes 3145728 | tf_op jit(solution)/shard_map/all_to_all | solution.py:81
  59.4 110.5 %reduce-scatter.8.cloned.1.call-start = ((), (), s32[]{:S(2)}) async-start(), calls=%async_computation.9 | async-start | bytes 2654208 | tf_op jit(solution)/shard_map/reduce_scatter | solution.py:101
  63.4 4.5 %copy-start.3 = (bf16[4,256,768]{1,2,0:T(8,128)(2,1)S(1)}, bf16[4,256,768]{1,2,0:T(8,128)(2,1)}, u32[]{:S(2)}) copy-start(bf16[4,256,768]{1,2,0:T(8,128)(2,1)} %copy.60) | copy-start | bytes 4718596
  63.4 4.5 %copy-start.4 = (bf16[4,768,384]{2,1,0:T(8,128)(2,1)S(1)}, bf16[4,768,384]{2,1,0:T(8,128)(2,1)}, u32[]{:S(2)}) copy-start(bf16[4,768,384]{2,1,0:T(8,128)(2,1)} %param.11) | copy-start | bytes 7077892
  83.3 5.8 %copy-start.6 = (bf16[4,256,768]{1,2,0:T(8,128)(2,1)S(1)}, bf16[4,256,768]{1,2,0:T(8,128)(2,1)}, u32[]{:S(2)}) copy-start(bf16[4,256,768]{1,2,0:T(8,128)(2,1)} %copy.62) | copy-start | bytes 4718596
  88.2 1.0 copy-start.7
  91.6 143.2 %reduce-scatter.6.cloned.1.call-start = ((), (), s32[]{:S(2)}) async-start(), calls=%async_computation.8 | async-start | bytes 2654208 | tf_op jit(solution)/shard_map/reduce_scatter | solution.py:98
  95.7 211.9 %reduce-scatter.4.cloned.1.call-start = ((), (), s32[]{:S(2)}) async-start(), calls=%async_computation.7 | async-start | bytes 2654208 | tf_op jit(solution)/shard_map/reduce_scatter | solution.py:95
  104.1 24.5 %all-to-all-start.1 = ((bf16[4,256,768]{2,0,1:T(4,128)(2,1)}), bf16[4,256,768]{2,0,1:T(4,128)(2,1)}, u32[]{:S(2)}, u32[]{:S(2)}) async-start(bf16[4,256,768]{2,0,1:T(4,128)(2,1)} %copy.52), calls=%async_computation.1 | async-start | bytes 3145728 | tf_op jit(solution)/shard_map/all_to_all | solution.py:80
  108.5 2.9 copy-start.5
  108.5 2.9 copy-start.8
  128.6 24.7 %all-to-all-start.3 = ((bf16[4,256,768]{2,0,1:T(4,128)(2,1)}), bf16[4,256,768]{2,0,1:T(4,128)(2,1)}, u32[]{:S(2)}, u32[]{:S(2)}) async-start(bf16[4,256,768]{2,0,1:T(4,128)(2,1)} %copy.58), calls=%async_computation.3 | async-start | bytes 3145728 | tf_op jit(solution)/shard_map/all_to_all | solution.py:85
Sparse Core Ops, SparseCore 0:
  91.7 70.6 reduce-scatter.7
  166.0 68.7 reduce-scatter.5
  238.3 69.1 reduce-scatter.3
where the time goes:
time: 317 us; the launch traced here: 316 us
  waiting for transfers between devices  179 us (56%)
  local copies, waits for them, and re-layouts  53.7 us (17%)
  matrix products  27.8 us (9%)
  other arithmetic  23.2 us (7%)
  starting transfers between devices  18 us (6%)
  between operations  14 us (4%)
    reduce_scatter x1, waiting for transfers between devices, shards(): lax.psum_scatter(weight_gate.astype(jnp.bfloat16), 'dp', scatter_dimensio...  70.9 us
    reduce_scatter x1, waiting for transfers between devices, shards(): lax.psum_scatter(weight_up.astype(jnp.bfloat16), 'dp', scatter_dimension=...  63 us
    all_to_all x1, waiting for transfers between devices, shards(): lax.all_to_all(outputs, 'expert', split_axis=1, concat_axis=1, tiled=True)  13.8 us
    all_to_all x1, waiting for transfers between devices, shards(): lax.all_to_all(entry_grad, 'expert', split_axis=1, concat_axis=1, tiled=T...  11.3 us
    gather x3, local copies, waits for them, and re-layouts, combine(): returned.reshape(slots_all, d_model)[slot_index].astype(jnp.float32)  10.8 us
    all_to_all x1, waiting for transfers between devices, shards(): lax.all_to_all(send_rows, 'expert', split_axis=1, concat_axis=1, tiled=True)  10.6 us
    all_to_all x1, waiting for transfers between devices, shards(): lax.all_to_all(send_grads, 'expert', split_axis=1, concat_axis=1, tiled=T...  9.44 us
    reduce_sum x2, other arithmetic, combine(): jnp.sum((weights[:, None] * picked).reshape(tok_rows, top_count, d_model)...  7 us
  transfers between devices with their start and end apart: 7, of which 6 were waited for; matrix products, arithmetic and copies ran while one was open for 22% of the time, Pallas kernels for 0%

commit v1 on v0

v1 whole, which is shorter than its diff:
```python
import functools

import jax
import jax.numpy as jnp
from jax import lax
from jax.experimental import pallas as pl
from jax.experimental.pallas import tpu as pltpu
from jax.sharding import PartitionSpec as P

BF = jnp.bfloat16
F32 = jnp.float32


def dot(a, b, ca=1, cb=0):
    return lax.dot_general(a, b, (((ca,), (cb,)), ((), ())), preferred_element_type=F32)


def flipped(me, k):
    out, bit = me, 1
    while bit <= k:
        if k & bit:
            out = out + bit * (1 - 2 * lax.rem(lax.div(me, bit), 2))
        bit *= 2
    return out


def kernel(
    n, inner, outer, top, scale,
    meta, tok, cot, wg_h, wu_h, wd_h,
    out_o, din_o, gg_o, gu_o, gd_o,
    w, meta_r, tok_r, cot_r, hot, slot_gate, xs, gs, ys, ds, y_t, y_r, g_all, x_r, z_s, z_r,
    w_sem, ms_sem, mr_sem, ts_sem, tr_sem, cs_sem, cr_sem, ys_sem, yr_sem, xs_sem, xr_sem, zs_sem, zr_sem,
):
    me = lax.axis_index("expert")
    my_dp = lax.axis_index("dp")
    my_z = lax.div(my_dp, inner)
    my_x = lax.rem(my_dp, inner)
    local, d_model, ff = w.shape[1:]
    tokens = tok.shape[0]
    cap = slot_gate.shape[2]
    rows = g_all.shape[4]
    other_x = 1 - my_x
    partner_dp = my_z * inner + other_x

    def z_peer(k):
        return lax.rem(my_z + k, outer) * inner + my_x

    loads = [pltpu.make_async_copy(h, w.at[i], w_sem.at[i]) for i, h in enumerate((wg_h, wu_h, wd_h))]

    barrier = pltpu.get_barrier_semaphore()
    for k in range(1, n):
        pl.semaphore_signal(barrier, inc=1, device_id={"expert": flipped(me, k)})
    pl.semaphore_signal(barrier, inc=1, device_id={"dp": partner_dp})
    for k in range(1, outer):
        pl.semaphore_signal(barrier, inc=1, device_id={"dp": z_peer(k)})
    pl.semaphore_wait(barrier, (n - 1) + 1 + (outer - 1))

    def send(src, dst, s, r, **where):
        return pltpu.make_async_remote_copy(src_ref=src, dst_ref=dst, send_sem=s, recv_sem=r, device_id=where)

    def meta_copy(k):
        return send(meta, meta_r.at[k], ms_sem.at[k], mr_sem.at[k], expert=flipped(me, k))

    def rows_copy(own, landed, s, r, k):
        if k % 2 == 0 or k == 1:
            return send(own, landed.at[k], s.at[k], r.at[k], expert=flipped(me, k))
        return send(landed.at[k - 1], landed.at[k], s.at[k], r.at[k], expert=flipped(me, 1))

    def tok_copy(k):
        return rows_copy(tok, tok_r, ts_sem, tr_sem, k)

    def cot_copy(k):
        return rows_copy(cot, cot_r, cs_sem, cr_sem, k)

    for k in range(1, n):
        meta_copy(k).start()
    direct = [k for k in range(2, n, 2)] + [1]
    for k in direct:
        tok_copy(k).start()
    for k in direct:
        cot_copy(k).start()
    for c in loads:
        c.start()

    above = (
        lax.broadcasted_iota(jnp.int32, (tokens, tokens), 0)
        < lax.broadcasted_iota(jnp.int32, (tokens, tokens), 1)
    )
    before = jnp.where(above, 1.0, 0.0).astype(BF)
    padded = -(-local // 8) * 8

    def route(k):
        if k:
            meta_copy(k).wait_recv()
            mv = meta_r[k]
        else:
            mv = meta[...]
        expert = lax.broadcasted_iota(jnp.int32, (padded, tokens), 0) + me * local
        hit = jnp.zeros((padded, tokens), F32)
        gate = jnp.zeros((padded, tokens), F32)
        for c in range(top):
            same = mv[c : c + 1] == expert
            hit = hit + jnp.where(same, 1.0, 0.0)
            gate = gate + jnp.where(same, mv[top + c : top + c + 1].astype(F32) * (1.0 / 65536.0), 0.0)
        rank = dot(hit.astype(BF), before)
        rank = jnp.where(hit > 0.5, rank, -1.0)
        slot = lax.broadcasted_iota(jnp.int32, (cap, tokens), 0).astype(F32)
        for i in range(local):
            picked = jnp.where(slot == rank[i : i + 1], 1.0, 0.0)
            hot[k, i * cap : (i + 1) * cap] = picked.astype(BF)
            value = jnp.sum(picked * gate[i : i + 1], axis=1, keepdims=True)
            slot_gate[k, i] = jnp.broadcast_to(value, (cap, 128))

    def take_tokens(k, block):
        got = dot(hot[k], block).astype(BF)
        for i in range(local):
            xs[i, k * cap : (k + 1) * cap] = got[i * cap : (i + 1) * cap]

    def take_grads(k, block):
        got = dot(hot[k], block)
        for i in range(local):
            gs[i, k * cap : (k + 1) * cap] = (
                slot_gate[k, i][:, :1] * got[i * cap : (i + 1) * cap]
            ).astype(BF)

    def arrive(copy_of, take, landed):
        for k in range(2, n, 2):
            copy_of(k).wait_recv()
            copy_of(k + 1).start()
        for k in range(1, n):
            if k % 2 or k == 1:
                copy_of(k).wait_recv()
            take(k, landed[k])

    for k in range(n):
        route(k)
    take_tokens(0, tok[...])
    take_grads(0, cot[...])
    arrive(tok_copy, take_tokens, tok_r)
    arrive(cot_copy, take_grads, cot_r)
    for c in loads:
        c.wait()

    def x_copy(e, a):
        return send(
            g_all.at[other_x, e, a], x_r.at[e, a], xs_sem.at[e, a], xr_sem.at[e, a], dp=partner_dp
        )

    def put(e, a, value):
        for zz in range(outer):
            for xx in range(inner):
                at = (zz * inner + xx) * rows
                g_all[xx, e, a, zz] = value[at : at + rows].astype(BF)
        x_copy(e, a).start()

    def one_expert(e, carry):
        x, g = xs[e], gs[e]
        pre_gate = dot(x, w[0, e])
        pre_up = dot(x, w[1, e])
        sig = jax.nn.sigmoid(pre_gate)
        act = pre_gate * sig
        hidden = (act * pre_up).astype(BF)
        put(e, 2, dot(g, hidden, 0, 0))
        hidden_grad = dot(g, w[2, e])
        gate_grad = (hidden_grad * pre_up * sig * (1.0 + pre_gate * (1.0 - sig))).astype(BF)
        up_grad = (hidden_grad * act).astype(BF)
        put(e, 0, dot(x, gate_grad, 0, 0))
        put(e, 1, dot(x, up_grad, 0, 0))
        o = dot(hidden, w[2, e], 1, 1).astype(BF).astype(F32)
        back = dot(gate_grad, w[0, e], 1, 1) + dot(up_grad, w[1, e], 1, 1)
        back = back.astype(BF)
        for k in range(n):
            ys[k, e] = (slot_gate[k, e][:, :1] * o[k * cap : (k + 1) * cap]).astype(BF)
            ds[k, e] = back[k * cap : (k + 1) * cap]
        return carry

    lax.fori_loop(0, local, one_expert, 0)

    def y_copy(j, k):
        return send(y_t.at[j, k], y_r.at[j, k], ys_sem.at[j, k], yr_sem.at[j, k], expert=flipped(me, k))

    def spread(j, k):
        src = (ys, ds)[j]
        return dot(hot[k], src[k].reshape(local * cap, d_model), 0, 0)

    for j in range(2):
        for k in range(n - 1, 0, -1):
            y_t[j, k] = spread(j, k).astype(BF)
            y_copy(j, k).start()

    def z_copy(k, e, a):
        return send(
            z_s.at[e, a, lax.rem(my_z + k, outer)],
            z_r.at[outer - k, e, a],
            zs_sem.at[k, e, a],
            zr_sem.at[outer - k, e, a],
            dp=z_peer(k),
        )

    order = (2, 0, 1)

    def x_stage(e, carry):
        for a in order:
            x_copy(e, a).wait_recv()
            z_s[e, a] = (g_all[my_x, e, a].astype(F32) + x_r[e, a].astype(F32)).astype(BF)
            for k in range(1, outer):
                z_copy(k, e, a).start()
        return carry

    def finish(e, carry):
        for a, o_ref in ((2, gd_o), (0, gg_o), (1, gu_o)):
            total = z_s[e, a, my_z].astype(F32)
            for k in range(1, outer):
                z_copy(outer - k, e, a).wait_recv()
                total = total + z_r[k, e, a].astype(F32)
            o_ref[e] = total * scale
        return carry

    lax.fori_loop(0, local - 1, x_stage, 0)
    for j, o_ref in enumerate((out_o, din_o)):
        total = spread(j, 0)
        for k in range(1, n):
            y_copy(j, k).wait_recv()
            total = total + y_r[j, k].astype(F32)
        o_ref[...] = total.astype(BF)
    lax.fori_loop(0, local - 1, finish, 0)
    x_stage(local - 1, 0)
    finish(local - 1, 0)

    for k in range(1, n):
        meta_copy(k).wait_send()
        tok_copy(k).wait_send()
        cot_copy(k).wait_send()
        for j in range(2):
            y_copy(j, k).wait_send()

    def drain(e, carry):
        for a in range(3):
            x_copy(e, a).wait_send()
            for k in range(1, outer):
                z_copy(k, e, a).wait_send()
        return carry

    lax.fori_loop(0, local, drain, 0)


def shards(tokens, expert_ids, gate_fixed, cotangent, w_gate, w_up, w_down):
    n = lax.axis_size("expert")
    replicas = lax.axis_size("dp")
    inner = 2
    outer = replicas // inner
    local, d_model, ff = w_gate.shape
    count, top = expert_ids.shape
    cap = count * top * 2 // (local * n)
    rows = d_model // replicas
    scale = float(count * n * replicas * top // (local * n)) ** (-0.5)
    meta = jnp.concatenate(
        [expert_ids.T, gate_fixed.T, jnp.zeros((8 - 2 * top, count), jnp.int32)], axis=0
    )
    vmem = pl.BlockSpec(memory_space=pltpu.VMEM)
    hbm = pl.BlockSpec(memory_space=pl.ANY)
    dma = pltpu.SemaphoreType.DMA
    block = jax.ShapeDtypeStruct((count, d_model), BF)
    grad = jax.ShapeDtypeStruct((local, rows, ff), F32)
    return pl.pallas_call(
        functools.partial(kernel, n, inner, outer, top, scale),
        out_shape=(block, block, grad, grad, grad),
        in_specs=[vmem] * 3 + [hbm] * 3,
        out_specs=(vmem,) * 5,
        scratch_shapes=[
            pltpu.VMEM((3, local, d_model, ff), BF),
            pltpu.VMEM((n, 8, count), jnp.int32),
            pltpu.VMEM((n, count, d_model), BF),
            pltpu.VMEM((n, count, d_model), BF),
            pltpu.VMEM((n, local * cap, count), BF),
            pltpu.VMEM((n, local, cap, 128), F32),
            pltpu.VMEM((local, n * cap, d_model), BF),
            pltpu.VMEM((local, n * cap, d_model), BF),
            pltpu.VMEM((n, local, cap, d_model), BF),
            pltpu.VMEM((n, local, cap, d_model), BF),
            pltpu.VMEM((2, n, count, d_model), BF),
            pltpu.VMEM((2, n, count, d_model), BF),
            pltpu.VMEM((inner, local, 3, outer, rows, ff), BF),
            pltpu.VMEM((local, 3, outer, rows, ff), BF),
            pltpu.VMEM((local, 3, outer, rows, ff), BF),
            pltpu.VMEM((outer, local, 3, rows, ff), BF),
            dma((3,)),
            dma((n,)), dma((n,)), dma((n,)), dma((n,)), dma((n,)), dma((n,)),
            dma((2, n)), dma((2, n)),
            dma((local, 3)), dma((local, 3)),
            dma((outer, local, 3)), dma((outer, local, 3)),
        ],
        compiler_params=pltpu.CompilerParams(
            collective_id=0, has_side_effects=True, vmem_limit_bytes=60 * 1024 * 1024
        ),
    )(meta, tokens, cotangent, w_gate, w_up, w_down)


def solution(mesh):
    return jax.shard_map(
        shards,
        mesh=mesh,
        in_specs=(P(("dp", "expert"), None),) * 4 + (P("expert", None, None),) * 3,
        out_specs=(P(("dp", "expert"), None),) * 2 + (P("expert", "dp", None),) * 3,
        check_vma=False,
    )
```

time: 317 us -> 129 us (0.41)
  waiting for transfers between devices: 179 us -> 0 us
  Pallas kernels: 0 us -> 119 us
  local copies, waits for them, and re-layouts: 53.7 us -> 7.26 us
  matrix products: 27.8 us -> 0 us
  other arithmetic: 23.2 us -> 1.37 us
  starting transfers between devices: 18 us -> 0 us
  between operations: 14 us -> 0.67 us
    reduce_scatter x3 -> x0, waiting for transfers between devices: 134 us -> none  [the longest x1 70.9 us: shards(): lax.psum_scatter(weight_gate.astype(jnp.bfloat16), 'dp', scatter_dimensio...]
    pallas_call x0 -> x1, Pallas kernels: none -> 119 us  [shards(): pl.pallas_call(functools.partial(kernel, n, inner, outer, top, scale), ou...]
    all_to_all x4 -> x0, waiting for transfers between devices: 45.1 us -> none  [the longest x1 13.8 us: shards(): lax.all_to_all(outputs, 'expert', split_axis=1, concat_axis=1, tiled=True)]
    gather x6 -> x0, local copies, waits for them, and re-layouts: 28.1 us -> none  [the longest x3 10.8 us: combine(): returned.reshape(slots_all, d_model)[slot_index].astype(jnp.float32)]
    dot_general x9 -> x0, matrix products: 27.8 us -> none  [the longest x1 4.85 us: expert_backward(): jnp.einsum('erd,edf->erf', grads_in, w_down, preferred_element_type=jnp.f...]
    all_to_all x4 -> x0, starting transfers between devices: 17.7 us -> none  [the longest x1 4.57 us: shards(): lax.all_to_all(entry_grad, 'expert', split_axis=1, concat_axis=1, tiled=T...]
    all_to_all x4 -> x0, local copies, waits for them, and re-layouts: 13.2 us -> none  [the longest x1 3.77 us: shards(): lax.all_to_all(send_grads, 'expert', split_axis=1, concat_axis=1, tiled=T...]
    convert_element_type x6 -> x0, other arithmetic: 10.4 us -> none  [the longest x3 5.44 us: shards(): grad_gate, grad_up, grad_down = (lax.psum_scatter(weight_gate.astype(jnp....]
  transfers between devices with their start and end apart: 7 -> 0, of which waited for: 6 -> 0; matrix products, arithmetic and copies ran while one was open for 22% -> 0% of each run, Pallas kernels for 0% -> 0%
where the time goes in v1:
time: 129 us; the launch traced here: 128 us
  Pallas kernels  119 us (92%)
  local copies, waits for them, and re-layouts  7.26 us (6%)
  other arithmetic  1.37 us (1%)
    pallas_call x1, Pallas kernels, shards(): pl.pallas_call(functools.partial(kernel, n, inner, outer, top, scale), ou...  119 us
    unnamed x9, local copies, waits for them, and re-layouts  7.18 us

profile of v1, /device:TPU:0, one launch (start us, length us, event | category | flops | bytes accessed | tf_op | source)
XLA Modules:
  0.0 128.1 jit_solution(9502056664154142672)
XLA Ops:
  0.6 0.1 pad.2.clone
  0.7 1.4 %add_add_fusion.meta = s32[8,256]{1,0:T(8,128)} fusion(s32[2,256]{1,0:T(2,128)} %bitcast.2, s32[2,256]{1,0:T(2,128)} %bitcast.3, s32[8]{0:T(128)S(1)} %pad.2.clone), kind=kLoop, calls=%fused_computation | loop fusion | flops 4096 | bytes 12320 | tf_op jit(solution)/shard_map/concatenate | solution.py:257
  2.1 118.8 %shard_map.110 = (bf16[256,768]{1,0:T(8,128)(2,1)}, bf16[256,768]{1,0:T(8,128)(2,1)}, f32[4,96,384]{2,1,0:T(8,128)}, f32[4,96,384]{2,1,0:T(8,128)}, f32[4,96,384]{2,1,0:T(8,128)}) custom-call(s32[8,256]{1,0:T(8,128)} %add_add_fusion.meta, bf16[256,768]{1,0:T(8,128)(2,1)} %tok.1, bf16[256,768]{1,0:T(8,128)(2,1)} %cot.1, bf16[4,768,384]{2,1,0:T(8,128)(2,1)} %wg_h.1, ...), custom_call_target="tpu_custom_call" | custom-call | tf_op jit(solution)/shard_map/pallas_call | solution.py:265
  120.9 0.0 copy-start.1
  120.9 0.0 copy-start
  120.9 1.9 %copy.17 = bf16[256,768]{1,0:T(8,128)(2,1)} copy(bf16[256,768]{1,0:T(8,128)(2,1)} %get-tuple-element.10) | data formatting | bytes 786432
  122.7 1.8 %copy.18 = bf16[256,768]{1,0:T(8,128)(2,1)} copy(bf16[256,768]{1,0:T(8,128)(2,1)} %get-tuple-element.11) | data formatting | bytes 786432
  124.5 1.9 %copy.19 = f32[4,96,384]{2,1,0:T(8,128)} copy(f32[4,96,384]{2,1,0:T(8,128)} %get-tuple-element.12) | data formatting | bytes 1179648
  126.4 0.0 copy-done.1
  126.4 0.8 copy.20
  127.2 0.0 copy-done
  127.2 0.8 copy.21
  (1 shorter events, 0.0 us)
Async XLA Ops:
  120.9 5.6 %copy-start.1 = (f32[4,96,384]{2,1,0:T(8,128)S(1)}, f32[4,96,384]{2,1,0:T(8,128)}, u32[]{:S(2)}) copy-start(f32[4,96,384]{2,1,0:T(8,128)} %get-tuple-element.13) | copy-start | bytes 1769476
  120.9 6.4 %copy-start = (f32[4,96,384]{2,1,0:T(8,128)S(1)}, f32[4,96,384]{2,1,0:T(8,128)}, u32[]{:S(2)}) copy-start(f32[4,96,384]{2,1,0:T(8,128)} %get-tuple-element.14) | copy-start | bytes 1769476

commit v2 on v1

v2 whole, which is shorter than its diff:
```python
import functools

import jax
import jax.numpy as jnp
from jax import lax
from jax.experimental import pallas as pl
from jax.experimental.pallas import tpu as pltpu
from jax.sharding import PartitionSpec as P

BF = jnp.bfloat16
F32 = jnp.float32


def dot(a, b, ca=1, cb=0):
    return lax.dot_general(a, b, (((ca,), (cb,)), ((), ())), preferred_element_type=F32)


def flipped(me, k):
    out, bit = me, 1
    while bit <= k:
        if k & bit:
            out = out + bit * (1 - 2 * lax.rem(lax.div(me, bit), 2))
        bit *= 2
    return out


def bit_of(i, b):
    return lax.rem(lax.div(i, 1 << b), 2)


def kernel(
    n, orders, top,
    meta, tok, cot, wg_h, wu_h, wd_h,
    act_o, grad_o,
    w, meta_r, tok_r, cot_r, hot, slot_gate, xs, gs, hs, pre, ys, ds, y_t, y_r, parts,
    w_sem, ms_sem, mr_sem, ts_sem, tr_sem, cs_sem, cr_sem, ys_sem, yr_sem, rs_sem, rr_sem,
    *halves,
):
    bits = len(orders[0])
    landed_at, summed = halves[:bits], halves[bits:]
    me = lax.axis_index("expert")
    my_dp = lax.axis_index("dp")
    local, d_model, ff = w.shape[1:]
    tokens = tok.shape[0]
    cap = slot_gate.shape[2]
    rows = parts.shape[3]

    loads = [pltpu.make_async_copy(h, w.at[i], w_sem.at[i]) for i, h in enumerate((wg_h, wu_h, wd_h))]

    barrier = pltpu.get_barrier_semaphore()
    for k in range(1, n):
        pl.semaphore_signal(barrier, inc=1, device_id={"expert": flipped(me, k)})
    for b in range(bits):
        pl.semaphore_signal(barrier, inc=1, device_id={"dp": flipped(my_dp, 1 << b)})
    pl.semaphore_wait(barrier, (n - 1) + bits)

    def send(src, dst, s, r, **where):
        return pltpu.make_async_remote_copy(src_ref=src, dst_ref=dst, send_sem=s, recv_sem=r, device_id=where)

    def meta_copy(k):
        return send(meta, meta_r.at[k], ms_sem.at[k], mr_sem.at[k], expert=flipped(me, k))

    def rows_copy(own, landed, s, r, k):
        if k % 2 == 0 or k == 1:
            return send(own, landed.at[k], s.at[k], r.at[k], expert=flipped(me, k))
        return send(landed.at[k - 1], landed.at[k], s.at[k], r.at[k], expert=flipped(me, 1))

    def tok_copy(k):
        return rows_copy(tok, tok_r, ts_sem, tr_sem, k)

    def cot_copy(k):
        return rows_copy(cot, cot_r, cs_sem, cr_sem, k)

    for k in range(1, n):
        meta_copy(k).start()
    direct = [k for k in range(2, n, 2)] + [1]
    for k in direct:
        tok_copy(k).start()
    for k in direct:
        cot_copy(k).start()
    for c in loads:
        c.start()

    above = (
        lax.broadcasted_iota(jnp.int32, (tokens, tokens), 0)
        < lax.broadcasted_iota(jnp.int32, (tokens, tokens), 1)
    )
    before = jnp.where(above, 1.0, 0.0).astype(BF)
    padded = -(-local // 8) * 8

    def route(k):
        if k:
            meta_copy(k).wait_recv()
            mv = meta_r[k]
        else:
            mv = meta[...]
        expert = lax.broadcasted_iota(jnp.int32, (padded, tokens), 0) + me * local
        hit = jnp.zeros((padded, tokens), F32)
        gate = jnp.zeros((padded, tokens), F32)
        for c in range(top):
            same = mv[c : c + 1] == expert
            hit = hit + jnp.where(same, 1.0, 0.0)
            gate = gate + jnp.where(same, mv[top + c : top + c + 1].astype(F32) * (1.0 / 65536.0), 0.0)
        rank = dot(hit.astype(BF), before)
        rank = jnp.where(hit > 0.5, rank, -1.0)
        slot = lax.broadcasted_iota(jnp.int32, (cap, tokens), 0).astype(F32)
        for i in range(local):
            picked = jnp.where(slot == rank[i : i + 1], 1.0, 0.0)
            hot[k, i * cap : (i + 1) * cap] = picked.astype(BF)
            value = jnp.sum(picked * gate[i : i + 1], axis=1, keepdims=True)
            slot_gate[k, i] = jnp.broadcast_to(value, (cap, 128))

    def take_tokens(k, block):
        got = dot(hot[k], block).astype(BF)
        for i in range(local):
            xs[i, k * cap : (k + 1) * cap] = got[i * cap : (i + 1) * cap]

    def take_grads(k, block):
        got = dot(hot[k], block)
        for i in range(local):
            gs[i, k * cap : (k + 1) * cap] = (
                slot_gate[k, i][:, :1] * got[i * cap : (i + 1) * cap]
            ).astype(BF)

    def arrive(copy_of, take, landed):
        for k in range(2, n, 2):
            copy_of(k).wait_recv()
            copy_of(k + 1).start()
        for k in range(1, n):
            if k % 2 or k == 1:
                copy_of(k).wait_recv()
            take(k, landed[k])

    def halve(s, e, a):
        b = orders[a][s]
        held = parts if s == 0 else summed[s - 1]
        half = 1 << (bits - 1 - s)
        return send(
            held.at[e, a, pl.ds((1 - bit_of(my_dp, b)) * half, half)],
            landed_at[s].at[e, a],
            rs_sem.at[s, e, a],
            rr_sem.at[s, e, a],
            dp=flipped(my_dp, 1 << b),
        )

    def put(e, a, value):
        for c in range(1 << bits):
            at = sum(((c >> b) & 1) << (bits - 1 - p) for p, b in enumerate(orders[a]))
            parts[e, a, at] = value[c * rows : (c + 1) * rows].astype(BF)
        halve(0, e, a).start()

    def forward(e, carry):
        x = xs[e]
        pre_gate = dot(x, w[0, e])
        pre_up = dot(x, w[1, e])
        pre[0, e] = pre_gate
        pre[1, e] = pre_up
        hidden = (pre_gate * jax.nn.sigmoid(pre_gate) * pre_up).astype(BF)
        hs[e] = hidden
        o = dot(hidden, w[2, e], 1, 1).astype(BF).astype(F32)
        for k in range(n):
            ys[k, e] = (slot_gate[k, e][:, :1] * o[k * cap : (k + 1) * cap]).astype(BF)
        return carry

    def backward(e, carry):
        x, g = xs[e], gs[e]
        put(e, 2, dot(g, hs[e], 0, 0))
        hidden_grad = dot(g, w[2, e])
        pre_gate, pre_up = pre[0, e], pre[1, e]
        sig = jax.nn.sigmoid(pre_gate)
        up_grad = (hidden_grad * (pre_gate * sig)).astype(BF)
        put(e, 1, dot(x, up_grad, 0, 0))
        gate_grad = (hidden_grad * pre_up * sig * (1.0 + pre_gate * (1.0 - sig))).astype(BF)
        put(e, 0, dot(x, gate_grad, 0, 0))
        back = dot(gate_grad, w[0, e], 1, 1) + dot(up_grad, w[1, e], 1, 1)
        back = back.astype(BF)
        for k in range(n):
            ds[k, e] = back[k * cap : (k + 1) * cap]
        return carry

    for k in range(n):
        route(k)
    take_tokens(0, tok[...])
    take_grads(0, cot[...])
    arrive(tok_copy, take_tokens, tok_r)
    for c in loads:
        c.wait()
    lax.fori_loop(0, local, forward, 0)
    arrive(cot_copy, take_grads, cot_r)
    lax.fori_loop(0, local, backward, 0)

    def y_copy(j, k):
        return send(y_t.at[j, k], y_r.at[j, k], ys_sem.at[j, k], yr_sem.at[j, k], expert=flipped(me, k))

    def spread(j, k):
        src = (ys, ds)[j]
        return dot(hot[k], src[k].reshape(local * cap, d_model), 0, 0)

    for j in range(2):
        for k in range(n - 1, 0, -1):
            y_t[j, k] = spread(j, k).astype(BF)
            y_copy(j, k).start()

    def total_of(s, e, a):
        halve(s, e, a).wait_recv()
        held = parts if s == 0 else summed[s - 1]
        half = 1 << (bits - 1 - s)
        mine = held[e, a, pl.ds(bit_of(my_dp, orders[a][s]) * half, half)]
        return mine.astype(F32) + landed_at[s][e, a].astype(F32)

    def step(s, e, a):
        summed[s][e, a] = total_of(s, e, a).astype(BF)
        halve(s + 1, e, a).start()

    def finish(e, a):
        grad_o[a, e] = total_of(bits - 1, e, a)[0]

    def returned(j):
        total = spread(j, 0)
        for k in range(1, n):
            y_copy(j, k).wait_recv()
            total = total + y_r[j, k].astype(F32)
        act_o[j] = total.astype(BF)

    events = []
    first = [(e, a) for e in range(local) for a in (2, 0)]
    other = [(e, 1) for e in range(local)]
    for i, (e, a) in enumerate(first):
        at = i + 1.0
        for s in range(bits):
            events.append((at, step if s < bits - 1 else finish, s, e, a))
            at = (max(at, float(len(other))) if s == 0 else at) + 0.6 / (1 << s)
    for i, (e, a) in enumerate(other):
        at = i + 1.0
        for s in range(bits):
            events.append((at, step if s < bits - 1 else finish, s, e, a))
            at = (len(first) + 0.5 * (i + 1) if s == 0 else at + 0.5 / (1 << s))
    events += [(0.6 * len(first), returned, 0, 0, 0), (0.85 * len(first), returned, 0, 1, 0)]
    for _, what, s, e, a in sorted(events, key=lambda event: event[0]):
        if what is step:
            step(s, e, a)
        elif what is finish:
            finish(e, a)
        else:
            returned(e)

    for k in range(1, n):
        meta_copy(k).wait_send()
        tok_copy(k).wait_send()
        cot_copy(k).wait_send()
        for j in range(2):
            y_copy(j, k).wait_send()

    def drain(e, carry):
        for a in range(3):
            for s in range(bits):
                halve(s, e, a).wait_send()
        return carry

    lax.fori_loop(0, local, drain, 0)


def write(scale, act, grad, out_o, din_o, gg_o, gu_o, gd_o):
    out_o[...] = act[0]
    din_o[...] = act[1]
    for a, o in enumerate((gg_o, gu_o, gd_o)):
        o[...] = grad[a] * scale


def shards(tokens, expert_ids, gate_fixed, cotangent, w_gate, w_up, w_down):
    n = lax.axis_size("expert")
    replicas = lax.axis_size("dp")
    bits = replicas.bit_length() - 1
    straight = tuple(range(bits))
    swapped = straight[:2][::-1] + straight[2:]
    orders = (straight, swapped, straight)
    local, d_model, ff = w_gate.shape
    count, top = expert_ids.shape
    cap = count * top * 2 // (local * n)
    rows = d_model // replicas
    scale = float(count * n * replicas * top // (local * n)) ** (-0.5)
    meta = jnp.concatenate(
        [expert_ids.T, gate_fixed.T, jnp.zeros((8 - 2 * top, count), jnp.int32)], axis=0
    )
    vmem = pl.BlockSpec(memory_space=pltpu.VMEM)
    hbm = pl.BlockSpec(memory_space=pl.ANY)
    dma = pltpu.SemaphoreType.DMA
    halves = [pltpu.VMEM((local, 3, 1 << (bits - 1 - s), rows, ff), BF) for s in range(bits)]
    act, grad = pl.pallas_call(
        functools.partial(kernel, n, orders, top),
        out_shape=(
            jax.ShapeDtypeStruct((2, count, d_model), BF),
            jax.ShapeDtypeStruct((3, local, rows, ff), F32),
        ),
        in_specs=[vmem] * 3 + [hbm] * 3,
        out_specs=(vmem,) * 2,
        scratch_shapes=[
            pltpu.VMEM((3, local, d_model, ff), BF),
            pltpu.VMEM((n, 8, count), jnp.int32),
            pltpu.VMEM((n, count, d_model), BF),
            pltpu.VMEM((n, count, d_model), BF),
            pltpu.VMEM((n, local * cap, count), BF),
            pltpu.VMEM((n, local, cap, 128), F32),
            pltpu.VMEM((local, n * cap, d_model), BF),
            pltpu.VMEM((local, n * cap, d_model), BF),
            pltpu.VMEM((local, n * cap, ff), BF),
            pltpu.VMEM((2, local, n * cap, ff), F32),
            pltpu.VMEM((n, local, cap, d_model), BF),
            pltpu.VMEM((n, local, cap, d_model), BF),
            pltpu.VMEM((2, n, count, d_model), BF),
            pltpu.VMEM((2, n, count, d_model), BF),
            pltpu.VMEM((local, 3, replicas, rows, ff), BF),
            dma((3,)),
            dma((n,)), dma((n,)), dma((n,)), dma((n,)), dma((n,)), dma((n,)),
            dma((2, n)), dma((2, n)),
            dma((bits, local, 3)), dma((bits, local, 3)),
            *halves, *halves[:-1],
        ],
        compiler_params=pltpu.CompilerParams(
            collective_id=0, has_side_effects=True, vmem_limit_bytes=60 * 1024 * 1024
        ),
    )(meta, tokens, cotangent, w_gate, w_up, w_down)
    step = count // local
    act_block = jax.ShapeDtypeStruct((count, d_model), BF)
    grad_block = jax.ShapeDtypeStruct((local, rows, ff), F32)
    row_spec = pl.BlockSpec((step, d_model), lambda i: (i, 0))
    grad_spec = pl.BlockSpec((1, rows, ff), lambda i: (i, 0, 0))
    return pl.pallas_call(
        functools.partial(write, scale),
        grid=(local,),
        out_shape=(act_block, act_block, grad_block, grad_block, grad_block),
        in_specs=[
            pl.BlockSpec((2, step, d_model), lambda i: (0, i, 0)),
            pl.BlockSpec((3, 1, rows, ff), lambda i: (0, i, 0, 0)),
        ],
        out_specs=(row_spec, row_spec, grad_spec, grad_spec, grad_spec),
    )(act, grad)


def solution(mesh):
    return jax.shard_map(
        shards,
        mesh=mesh,
        in_specs=(P(("dp", "expert"), None),) * 4 + (P("expert", None, None),) * 3,
        out_specs=(P(("dp", "expert"), None),) * 2 + (P("expert", "dp", None),) * 3,
        check_vma=False,
    )
```

time: 129 us -> 136 us (1.054)
  Pallas kernels: 119 us -> 132 us
  local copies, waits for them, and re-layouts: 7.26 us -> 0.08 us
    pallas_call x1 -> x2, Pallas kernels: 119 us -> 132 us  [the longest x1 128 us: shards(): pl.pallas_call(functools.partial(kernel, n, orders, top), out_shape=(jax....]
    unnamed x9 -> x0, local copies, waits for them, and re-layouts: 7.18 us -> none
where the time goes in v2:
time: 136 us; the launch traced here: 134 us
  Pallas kernels  132 us (97%)
  other arithmetic  1.37 us (1%)
    pallas_call x1, Pallas kernels, shards(): pl.pallas_call(functools.partial(kernel, n, orders, top), out_shape=(jax....  128 us
    pallas_call x1, Pallas kernels, shards(): pl.pallas_call(functools.partial(write, scale), grid=(local,), out_shape=...  4 us

profile of v2, /device:TPU:0, one launch (start us, length us, event | category | flops | bytes accessed | tf_op | source)
XLA Modules:
  0.0 133.7 jit_solution(11441225995472223070)
XLA Ops:
  0.6 0.1 pad.2.clone
  0.7 1.4 %add_add_fusion.meta = s32[8,256]{1,0:T(8,128)} fusion(s32[2,256]{1,0:T(2,128)} %bitcast.2, s32[2,256]{1,0:T(2,128)} %bitcast.3, s32[8]{0:T(128)S(1)} %pad.2.clone), kind=kLoop, calls=%fused_computation | loop fusion | flops 4096 | bytes 12320 | tf_op jit(solution)/shard_map/concatenate | solution.py:282
  2.1 127.6 %shard_map.110 = (bf16[2,256,768]{2,1,0:T(8,128)(2,1)}, f32[3,4,96,384]{3,2,1,0:T(8,128)}) custom-call(s32[8,256]{1,0:T(8,128)} %add_add_fusion.meta, bf16[256,768]{1,0:T(8,128)(2,1)} %tok.1, bf16[256,768]{1,0:T(8,128)(2,1)} %cot.1, bf16[4,768,384]{2,1,0:T(8,128)(2,1)} %wg_h.1, bf16[4,768,384]{2,1,0:T(8,128)(2,1)} %wu_h.1, bf16[4,768,384]{2,1,0:T(8,128)(2,1)} %wd_h.1), custom_call_target="tpu_custom_call" | custom-call | tf_op jit(solution)/shard_map/pallas_call | solution.py:289
  129.7 4.0 %shard_map.111 = (bf16[256,768]{1,0:T(8,128)(2,1)}, bf16[256,768]{1,0:T(8,128)(2,1)}, f32[4,96,384]{2,1,0:T(8,128)}, f32[4,96,384]{2,1,0:T(8,128)}, f32[4,96,384]{2,1,0:T(8,128)}) custom-call(bf16[2,256,768]{2,1,0:T(8,128)(2,1)} %get-tuple-element.7.act, f32[3,4,96,384]{3,2,1,0:T(8,128)} %get-tuple-element.8.grad), custom_call_target="tpu_custom_call" | custom-call | tf_op jit(solution)/shard_map/pallas_call | solution.py:328
  (1 shorter events, 0.0 us)

commit v3 on v2

--- a/solution.py
+++ b/solution.py
@@ -24,35 +24,34 @@
     return out
 
 
-def bit_of(i, b):
-    return lax.rem(lax.div(i, 1 << b), 2)
-
-
 def kernel(
-    n, orders, top,
+    n, inner, outer, top,
     meta, tok, cot, wg_h, wu_h, wd_h,
     act_o, grad_o,
     w, meta_r, tok_r, cot_r, hot, slot_gate, xs, gs, hs, pre, ys, ds, y_t, y_r, parts,
-    w_sem, ms_sem, mr_sem, ts_sem, tr_sem, cs_sem, cr_sem, ys_sem, yr_sem, rs_sem, rr_sem,
-    *halves,
+    w_sem, ms_sem, mr_sem, ts_sem, tr_sem, cs_sem, cr_sem, ys_sem, yr_sem, xs_sem, xr_sem, zs_sem, zr_sem,
+    x_r, z_s, z_r,
 ):
-    bits = len(orders[0])
-    landed_at, summed = halves[:bits], halves[bits:]
     me = lax.axis_index("expert")
     my_dp = lax.axis_index("dp")
+    my_z = lax.div(my_dp, inner)
+    my_x = lax.rem(my_dp, inner)
+    other_x = 1 - my_x
+    partner_dp = my_z * inner + other_x
     local, d_model, ff = w.shape[1:]
     tokens = tok.shape[0]
     cap = slot_gate.shape[2]
-    rows = parts.shape[3]
+    rows = parts.shape[4]
 
     loads = [pltpu.make_async_copy(h, w.at[i], w_sem.at[i]) for i, h in enumerate((wg_h, wu_h, wd_h))]
 
     barrier = pltpu.get_barrier_semaphore()
     for k in range(1, n):
         pl.semaphore_signal(barrier, inc=1, device_id={"expert": flipped(me, k)})
-    for b in range(bits):
-        pl.semaphore_signal(barrier, inc=1, device_id={"dp": flipped(my_dp, 1 << b)})
-    pl.semaphore_wait(barrier, (n - 1) + bits)
+    pl.semaphore_signal(barrier, inc=1, device_id={"dp": partner_dp})
+    for k in range(1, outer):
+        pl.semaphore_signal(barrier, inc=1, device_id={"dp": flipped(my_z, k) * inner + my_x})
+    pl.semaphore_wait(barrier, (n - 1) + 1 + (outer - 1))
 
     def send(src, dst, s, r, **where):
         return pltpu.make_async_remote_copy(src_ref=src, dst_ref=dst, send_sem=s, recv_sem=r, device_id=where)
@@ -131,23 +130,24 @@
                 copy_of(k).wait_recv()
             take(k, landed[k])
 
-    def halve(s, e, a):
-        b = orders[a][s]
-        held = parts if s == 0 else summed[s - 1]
-        half = 1 << (bits - 1 - s)
+    def x_copy(e, a):
         return send(
-            held.at[e, a, pl.ds((1 - bit_of(my_dp, b)) * half, half)],
-            landed_at[s].at[e, a],
-            rs_sem.at[s, e, a],
-            rr_sem.at[s, e, a],
-            dp=flipped(my_dp, 1 << b),
+            parts.at[other_x, e, a], x_r.at[e, a], xs_sem.at[e, a], xr_sem.at[e, a], dp=partner_dp
         )
 
+    def z_copy(k, e, a):
+        there = flipped(my_z, k)
+        return send(
+            z_s.at[e, a, there], z_r.at[k, e, a], zs_sem.at[k, e, a], zr_sem.at[k, e, a],
+            dp=there * inner + my_x,
+        )
+
     def put(e, a, value):
-        for c in range(1 << bits):
-            at = sum(((c >> b) & 1) << (bits - 1 - p) for p, b in enumerate(orders[a]))
-            parts[e, a, at] = value[c * rows : (c + 1) * rows].astype(BF)
-        halve(0, e, a).start()
+        for zz in range(outer):
+            for xx in range(inner):
+                at = (zz * inner + xx) * rows
+                parts[xx, e, a, zz] = value[at : at + rows].astype(BF)
+        x_copy(e, a).start()
 
     def forward(e, carry):
         x = xs[e]
@@ -201,19 +201,22 @@
             y_t[j, k] = spread(j, k).astype(BF)
             y_copy(j, k).start()
 
-    def total_of(s, e, a):
-        halve(s, e, a).wait_recv()
-        held = parts if s == 0 else summed[s - 1]
-        half = 1 << (bits - 1 - s)
-        mine = held[e, a, pl.ds(bit_of(my_dp, orders[a][s]) * half, half)]
-        return mine.astype(F32) + landed_at[s][e, a].astype(F32)
-
-    def step(s, e, a):
-        summed[s][e, a] = total_of(s, e, a).astype(BF)
-        halve(s + 1, e, a).start()
-
-    def finish(e, a):
-        grad_o[a, e] = total_of(bits - 1, e, a)[0]
+    def x_stage(e, carry):
+        for a in (2, 1, 0):
+            x_copy(e, a).wait_recv()
+            z_s[e, a] = (parts[my_x, e, a].astype(F32) + x_r[e, a].astype(F32)).astype(BF)
+            for k in range(outer - 1, 0, -1):
+                z_copy(k, e, a).start()
+        return carry
+
+    def finish(e, carry):
+        for a in (2, 1, 0):
+            total = z_s[e, a, my_z].astype(F32)
+            for k in range(1, outer):
+                z_copy(k, e, a).wait_recv()
+                total = total + z_r[k, e, a].astype(F32)
+            grad_o[a, e] = total
+        return carry
 
     def returned(j):
         total = spread(j, 0)
@@ -222,27 +225,13 @@
             total = total + y_r[j, k].astype(F32)
         act_o[j] = total.astype(BF)
 
-    events = []
-    first = [(e, a) for e in range(local) for a in (2, 0)]
-    other = [(e, 1) for e in range(local)]
-    for i, (e, a) in enumerate(first):
-        at = i + 1.0
-        for s in range(bits):
-            events.append((at, step if s < bits - 1 else finish, s, e, a))
-            at = (max(at, float(len(other))) if s == 0 else at) + 0.6 / (1 << s)
-    for i, (e, a) in enumerate(other):
-        at = i + 1.0
-        for s in range(bits):
-            events.append((at, step if s < bits - 1 else finish, s, e, a))
-            at = (len(first) + 0.5 * (i + 1) if s == 0 else at + 0.5 / (1 << s))
-    events += [(0.6 * len(first), returned, 0, 0, 0), (0.85 * len(first), returned, 0, 1, 0)]
-    for _, what, s, e, a in sorted(events, key=lambda event: event[0]):
-        if what is step:
-            step(s, e, a)
-        elif what is finish:
-            finish(e, a)
-        else:
-            returned(e)
+    lax.fori_loop(0, local - 1, x_stage, 0)
+    for j in range(2):
+        returned(j)
+    lax.fori_loop(0, local - 2, finish, 0)
+    x_stage(local - 1, 0)
+    finish(local - 2, 0)
+    finish(local - 1, 0)
 
     for k in range(1, n):
         meta_copy(k).wait_send()
@@ -253,8 +242,9 @@
 
     def drain(e, carry):
         for a in range(3):
-            for s in range(bits):
-                halve(s, e, a).wait_send()
+            x_copy(e, a).wait_send()
+            for k in range(1, outer):
+                z_copy(k, e, a).wait_send()
         return carry
 
     lax.fori_loop(0, local, drain, 0)
@@ -270,10 +260,8 @@
 def shards(tokens, expert_ids, gate_fixed, cotangent, w_gate, w_up, w_down):
     n = lax.axis_size("expert")
     replicas = lax.axis_size("dp")
-    bits = replicas.bit_length() - 1
-    straight = tuple(range(bits))
-    swapped = straight[:2][::-1] + straight[2:]
-    orders = (straight, swapped, straight)
+    inner = 2
+    outer = replicas // inner
     local, d_model, ff = w_gate.shape
     count, top = expert_ids.shape
     cap = count * top * 2 // (local * n)
@@ -285,9 +273,9 @@
     vmem = pl.BlockSpec(memory_space=pltpu.VMEM)
     hbm = pl.BlockSpec(memory_space=pl.ANY)
     dma = pltpu.SemaphoreType.DMA
-    halves = [pltpu.VMEM((local, 3, 1 << (bits - 1 - s), rows, ff), BF) for s in range(bits)]
+    half = pltpu.VMEM((local, 3, outer, rows, ff), BF)
     act, grad = pl.pallas_call(
-        functools.partial(kernel, n, orders, top),
+        functools.partial(kernel, n, inner, outer, top),
         out_shape=(
             jax.ShapeDtypeStruct((2, count, d_model), BF),
             jax.ShapeDtypeStruct((3, local, rows, ff), F32),
@@ -309,12 +297,13 @@
             pltpu.VMEM((n, local, cap, d_model), BF),
             pltpu.VMEM((2, n, count, d_model), BF),
             pltpu.VMEM((2, n, count, d_model), BF),
-            pltpu.VMEM((local, 3, replicas, rows, ff), BF),
+            pltpu.VMEM((inner, local, 3, outer, rows, ff), BF),
             dma((3,)),
             dma((n,)), dma((n,)), dma((n,)), dma((n,)), dma((n,)), dma((n,)),
             dma((2, n)), dma((2, n)),
-            dma((bits, local, 3)), dma((bits, local, 3)),
-            *halves, *halves[:-1],
+            dma((local, 3)), dma((local, 3)),
+            dma((outer, local, 3)), dma((outer, local, 3)),
+            half, half, pltpu.VMEM((outer, local, 3, rows, ff), BF),
         ],
         compiler_params=pltpu.CompilerParams(
             collective_id=0, has_side_effects=True, vmem_limit_bytes=60 * 1024 * 1024
@@ -323,17 +312,11 @@
     step = count // local
     act_block = jax.ShapeDtypeStruct((count, d_model), BF)
     grad_block = jax.ShapeDtypeStruct((local, rows, ff), F32)
-    row_spec = pl.BlockSpec((step, d_model), lambda i: (i, 0))
-    grad_spec = pl.BlockSpec((1, rows, ff), lambda i: (i, 0, 0))
     return pl.pallas_call(
         functools.partial(write, scale),
-        grid=(local,),
         out_shape=(act_block, act_block, grad_block, grad_block, grad_block),
-        in_specs=[
-            pl.BlockSpec((2, step, d_model), lambda i: (0, i, 0)),
-            pl.BlockSpec((3, 1, rows, ff), lambda i: (0, i, 0, 0)),
-        ],
-        out_specs=(row_spec, row_spec, grad_spec, grad_spec, grad_spec),
+        in_specs=[vmem] * 2,
+        out_specs=(vmem,) * 5,
     )(act, grad)
 
 

time: 136 us -> 123 us (0.904); the launches traced: 134 us -> 123 us
  Pallas kernels: 132 us -> 120 us
    pallas_call x2, Pallas kernels: 132 us -> 120 us  [the longest x1 117 us: shards(): pl.pallas_call(functools.partial(kernel, n, inner, outer, top), out_shape...]
where the time goes in v3:
time: 123 us
  Pallas kernels  120 us (98%)
  other arithmetic  1.37 us (1%)
    pallas_call x1, Pallas kernels, shards(): pl.pallas_call(functools.partial(kernel, n, inner, outer, top), out_shape...  117 us
    pallas_call x1, Pallas kernels, shards(): pl.pallas_call(functools.partial(write, scale), out_shape=(act_block, act...  3.25 us

profile of v3, /device:TPU:0, one launch (start us, length us, event | category | flops | bytes accessed | tf_op | source)
XLA Modules:
  0.0 122.6 jit_solution(2878900296538207400)
XLA Ops:
  0.6 0.1 pad.2.clone
  0.7 1.4 %add_add_fusion.meta = s32[8,256]{1,0:T(8,128)} fusion(s32[2,256]{1,0:T(2,128)} %bitcast.2, s32[2,256]{1,0:T(2,128)} %bitcast.3, s32[8]{0:T(128)S(1)} %pad.2.clone), kind=kLoop, calls=%fused_computation | loop fusion | flops 4096 | bytes 12320 | tf_op jit(solution)/shard_map/concatenate | solution.py:270
  2.1 117.2 %shard_map.110 = (bf16[2,256,768]{2,1,0:T(8,128)(2,1)}, f32[3,4,96,384]{3,2,1,0:T(8,128)}) custom-call(s32[8,256]{1,0:T(8,128)} %add_add_fusion.meta, bf16[256,768]{1,0:T(8,128)(2,1)} %tok.1, bf16[256,768]{1,0:T(8,128)(2,1)} %cot.1, bf16[4,768,384]{2,1,0:T(8,128)(2,1)} %wg_h.1, bf16[4,768,384]{2,1,0:T(8,128)(2,1)} %wu_h.1, bf16[4,768,384]{2,1,0:T(8,128)(2,1)} %wd_h.1), custom_call_target="tpu_custom_call" | custom-call | tf_op jit(solution)/shard_map/pallas_call | solution.py:277
  119.3 3.3 %shard_map.111 = (bf16[256,768]{1,0:T(8,128)(2,1)}, bf16[256,768]{1,0:T(8,128)(2,1)}, f32[4,96,384]{2,1,0:T(8,128)}, f32[4,96,384]{2,1,0:T(8,128)}, f32[4,96,384]{2,1,0:T(8,128)}) custom-call(bf16[2,256,768]{2,1,0:T(8,128)(2,1)} %get-tuple-element.7.act, f32[3,4,96,384]{3,2,1,0:T(8,128)} %get-tuple-element.8.grad), custom_call_target="tpu_custom_call" | custom-call | tf_op jit(solution)/shard_map/pallas_call | solution.py:315
  (1 shorter events, 0.0 us)

commit v4 on v3

--- a/solution.py
+++ b/solution.py
@@ -196,16 +196,11 @@
         src = (ys, ds)[j]
         return dot(hot[k], src[k].reshape(local * cap, d_model), 0, 0)
 
-    for j in range(2):
-        for k in range(n - 1, 0, -1):
-            y_t[j, k] = spread(j, k).astype(BF)
-            y_copy(j, k).start()
-
     def x_stage(e, carry):
         for a in (2, 1, 0):
             x_copy(e, a).wait_recv()
             z_s[e, a] = (parts[my_x, e, a].astype(F32) + x_r[e, a].astype(F32)).astype(BF)
-            for k in range(outer - 1, 0, -1):
+            for k in range(1, outer):
                 z_copy(k, e, a).start()
         return carry
 
@@ -225,7 +220,12 @@
             total = total + y_r[j, k].astype(F32)
         act_o[j] = total.astype(BF)
 
-    lax.fori_loop(0, local - 1, x_stage, 0)
+    x_stage(0, 0)
+    for j in range(2):
+        for k in range(n - 1, 0, -1):
+            y_t[j, k] = spread(j, k).astype(BF)
+            y_copy(j, k).start()
+    lax.fori_loop(1, local - 1, x_stage, 0)
     for j in range(2):
         returned(j)
     lax.fori_loop(0, local - 2, finish, 0)

time: 123 us -> 121 us (0.984)
    pallas_call x1, Pallas kernels: 117 us -> 116 us  [shards(): pl.pallas_call(functools.partial(kernel, n, inner, outer, top), out_shape...]
where the time goes in v4:
time: 121 us
  Pallas kernels  119 us (98%)
  other arithmetic  1.37 us (1%)
    pallas_call x1, Pallas kernels, shards(): pl.pallas_call(functools.partial(kernel, n, inner, outer, top), out_shape...  116 us
    pallas_call x1, Pallas kernels, shards(): pl.pallas_call(functools.partial(write, scale), out_shape=(act_block, act...  3.25 us

profile of v4, /device:TPU:0, one launch (start us, length us, event | category | flops | bytes accessed | tf_op | source)
XLA Modules:
  0.0 121.1 jit_solution(1208867945972647649)
XLA Ops:
  0.6 0.1 pad.2.clone
  0.7 1.4 %add_add_fusion.meta = s32[8,256]{1,0:T(8,128)} fusion(s32[2,256]{1,0:T(2,128)} %bitcast.2, s32[2,256]{1,0:T(2,128)} %bitcast.3, s32[8]{0:T(128)S(1)} %pad.2.clone), kind=kLoop, calls=%fused_computation | loop fusion | flops 4096 | bytes 12320 | tf_op jit(solution)/shard_map/concatenate | solution.py:270
  2.1 115.7 %shard_map.110 = (bf16[2,256,768]{2,1,0:T(8,128)(2,1)}, f32[3,4,96,384]{3,2,1,0:T(8,128)}) custom-call(s32[8,256]{1,0:T(8,128)} %add_add_fusion.meta, bf16[256,768]{1,0:T(8,128)(2,1)} %tok.1, bf16[256,768]{1,0:T(8,128)(2,1)} %cot.1, bf16[4,768,384]{2,1,0:T(8,128)(2,1)} %wg_h.1, bf16[4,768,384]{2,1,0:T(8,128)(2,1)} %wu_h.1, bf16[4,768,384]{2,1,0:T(8,128)(2,1)} %wd_h.1), custom_call_target="tpu_custom_call" | custom-call | tf_op jit(solution)/shard_map/pallas_call | solution.py:277
  117.8 3.3 %shard_map.111 = (bf16[256,768]{1,0:T(8,128)(2,1)}, bf16[256,768]{1,0:T(8,128)(2,1)}, f32[4,96,384]{2,1,0:T(8,128)}, f32[4,96,384]{2,1,0:T(8,128)}, f32[4,96,384]{2,1,0:T(8,128)}) custom-call(bf16[2,256,768]{2,1,0:T(8,128)(2,1)} %get-tuple-element.7.act, f32[3,4,96,384]{3,2,1,0:T(8,128)} %get-tuple-element.8.grad), custom_call_target="tpu_custom_call" | custom-call | tf_op jit(solution)/shard_map/pallas_call | solution.py:315
  (1 shorter events, 0.0 us)
